TPU v7x, 32 devices: a whole 2x2x4 slice. The times are simulated.
32 devices in a mesh: dp: 8 (over z, core), seq: 4 (over y, x).
Axes of the slice: x: 2, y: 2, z: 4, core: 2. Of those that a mesh axis runs over, the one named last changes fastest.
Arguments:
- tokens_in: bfloat16 [16384, 1024], P(('dp', 'seq')), may hold values from -6 to 6
- norm_attn: bfloat16 [1024], P('dp'), may hold values from 0.5 to 1.5
- w_query: bfloat16 [1024, 1024], P('dp'), may hold values from -0.1875 to 0.1875
- key_value_weight: bfloat16 [1024, 1024], P('dp'), may hold values from -0.1875 to 0.1875
- gain_query: bfloat16 [64], P('dp'), may hold values from 1 to 2
- gain_key: bfloat16 [64], P('dp'), may hold values from 1 to 2
- w_out: bfloat16 [1024, 1024], P('dp'), may hold values from -0.75 to 0.75
- norm_ffn: bfloat16 [1024], P('dp'), may hold values from 0.5 to 1.5
- w_gate: bfloat16 [1024, 4608], P(None, 'dp'), may hold values from -0.1875 to 0.1875
- w_up: bfloat16 [1024, 4608], P(None, 'dp'), may hold values from -0.1875 to 0.1875
- w_down: bfloat16 [4608, 1024], P('dp'), may hold values from -0.09375 to 0.09375
- cotangent: bfloat16 [16384, 1024], P(('dp', 'seq')), may hold values from -6 to 6
- segments: int32 [8, 2048], P('dp'), may hold values from 0 to 3, never falling along the last dimension, each value on 1 to 1024 neighbouring positions
- blocks: int32 [8, 16], P('dp'), may hold values from 0 to 15, each once within a row
Outputs:
- output: bfloat16 [16384, 1024], P(('dp', 'seq'))
- grad_tokens: float32 [16384, 1024], P(('dp', 'seq'))
- grad_norm_attn: float32 [1024], P('dp')
- grad_w_query: float32 [1024, 1024], P('dp')
- grad_w_keyval: float32 [1024, 1024], P('dp')
- grad_gain_query: float32 [64], P('dp')
- grad_gain_key: float32 [64], P('dp')
- grad_w_out: float32 [1024, 1024], P('dp')
- grad_norm_ffn: float32 [1024], P('dp')
- grad_w_gate: float32 [1024, 4608], P(None, 'dp')
- grad_w_up: float32 [1024, 4608], P(None, 'dp')
- grad_w_down: float32 [4608, 1024], P('dp')
Inputs may be any that keep to these rules, and one draw needn't show every extreme that they name: `segments`: in each row the document numbers never fall, all 4 documents occur, each covers 1 to 1024 places and the longest exactly 1024. `blocks`: each row holds every block number once.
All inputs are finite; a program needn't handle non-finite values.
Results may differ from a plain program's by a relative error of at most 0.025.
Values may be sent and summed in bfloat16 or wider, within the bound.
A program may use at most 192 MiB of HBM per device.

v0:
```python
import math
import jax
import jax.numpy as jnp
from jax import lax
from jax.sharding import PartitionSpec as P

QUERY_HEADS = 16
KEY_VALUE_HEADS = 8
HEAD_SIZE = 64
BLOCK = 128
QUERY_ROWS = 512
EPS = 1e-05
THETA = 1000000.0
MASKED = -1e30


def normed(tensor, gain_vec):
    factor = lax.rsqrt(jnp.mean(tensor * tensor, axis=-1, keepdims=True) + EPS)
    return tensor * factor * gain_vec


def norm_back(tensor, gain_vec, upstream):
    factor = lax.rsqrt(jnp.mean(tensor * tensor, axis=-1, keepdims=True) + EPS)
    unit_value = tensor * factor
    weighted = upstream * gain_vec
    grad_in = factor * (
        weighted - unit_value * jnp.mean(weighted * unit_value, axis=-1, keepdims=True)
    )
    return (grad_in, upstream * unit_value)


def rotate(tensor, angle_cos, angle_sin):
    half_dim = tensor.shape[-1] // 2
    front_half = tensor[..., :half_dim]
    back_half = tensor[..., half_dim:]
    return jnp.concatenate(
        [
            front_half * angle_cos - back_half * angle_sin,
            back_half * angle_cos + front_half * angle_sin,
        ],
        axis=-1,
    )


def angles(offsets, head_dim):
    half_dim = head_dim // 2
    frequency = jnp.exp(
        jnp.arange(half_dim, dtype=jnp.float32) * (-2.0 * math.log(THETA) / head_dim)
    )
    turned = offsets.astype(jnp.float32)[:, None] * frequency[None, :]
    return (jnp.cos(turned)[:, None, :], jnp.sin(turned)[:, None, :])


def layout(segment_row, order_row, block_len):
    length_all = segment_row.shape[0]
    places = jnp.arange(length_all, dtype=jnp.int32)
    seg_start = jnp.concatenate([jnp.ones((1,), dtype=bool), segment_row[1:] != segment_row[:-1]])
    starts = lax.cummax(jnp.where(seg_start, places, 0), axis=0)
    offsets = places - starts
    placed_tokens = (
        order_row[:, None] * block_len + jnp.arange(block_len, dtype=jnp.int32)[None, :]
    ).reshape(length_all)
    return (placed_tokens, segment_row[placed_tokens], offsets[placed_tokens])


def plain_product(left_op, right_op):
    return jnp.dot(left_op, right_op, preferred_element_type=jnp.float32)


def dot_right_t(left_op, right_op):
    return lax.dot_general(
        left_op, right_op, (((1,), (1,)), ((), ())), preferred_element_type=jnp.float32
    )


def dot_left_t(left_op, right_op):
    return lax.dot_general(
        left_op, right_op, (((0,), (0,)), ((), ())), preferred_element_type=jnp.float32
    )


def gate_back(gate_pre, up_pre, upstream):
    gate_sig = jax.nn.sigmoid(gate_pre)
    grad_gate = upstream * up_pre * gate_sig * (1.0 + gate_pre * (1.0 - gate_sig))
    grad_up = upstream * gate_pre * gate_sig
    return (grad_gate.astype(jnp.bfloat16), grad_up.astype(jnp.bfloat16))


def shards(
    tokens_in,
    norm_attn,
    w_query,
    key_value_weight,
    gain_query,
    gain_key,
    w_out,
    norm_ffn,
    w_gate,
    w_up,
    w_down,
    cotangent,
    segments,
    blocks,
):
    sequence_count = lax.axis_size("seq")
    seq_index = lax.axis_index("seq")
    token_rows = tokens_in.shape[0]
    group_rows = token_rows * sequence_count
    local_key_value = KEY_VALUE_HEADS // sequence_count
    repeat_factor = QUERY_HEADS // KEY_VALUE_HEADS
    factor = HEAD_SIZE ** (-0.5)
    count_blocks = group_rows // QUERY_ROWS
    attn_gain, query_w, key_value_matrix, query_gain, key_gain, out_w, ffn_gain = (
        lax.all_gather(norm_attn, "dp", axis=0, tiled=True),
        lax.all_gather(w_query, "dp", axis=0, tiled=True),
        lax.all_gather(key_value_weight, "dp", axis=0, tiled=True),
        lax.all_gather(gain_query, "dp", axis=0, tiled=True),
        lax.all_gather(gain_key, "dp", axis=0, tiled=True),
        lax.all_gather(w_out, "dp", axis=0, tiled=True),
        lax.all_gather(norm_ffn, "dp", axis=0, tiled=True),
    )
    attn_gain = attn_gain.astype(jnp.float32)
    query_gain = query_gain.astype(jnp.float32)
    key_gain = key_gain.astype(jnp.float32)
    ffn_gain = ffn_gain.astype(jnp.float32)
    placed_tokens, documents_for_rows, offsets = layout(segments[0], blocks[0], BLOCK)
    angle_cos, angle_sin = angles(
        lax.dynamic_slice_in_dim(offsets, seq_index * token_rows, token_rows, 0), HEAD_SIZE
    )
    hidden = tokens_in.astype(jnp.float32)
    normalized_input = normed(hidden, attn_gain).astype(jnp.bfloat16)
    query_raw = plain_product(normalized_input, query_w).reshape(token_rows, QUERY_HEADS, HEAD_SIZE)
    key_value_unrotated = plain_product(normalized_input, key_value_matrix).reshape(
        token_rows, KEY_VALUE_HEADS, 2, HEAD_SIZE
    )
    query_low = rotate(normed(query_raw, query_gain), angle_cos, angle_sin).astype(jnp.bfloat16)
    key_low = rotate(normed(key_value_unrotated[:, :, 0], key_gain), angle_cos, angle_sin).astype(
        jnp.bfloat16
    )
    key_value_reduced = jnp.stack(
        [key_low, key_value_unrotated[:, :, 1].astype(jnp.bfloat16)], axis=2
    )
    query_heads, keyval_heads = (
        lax.all_to_all(
            query_low.reshape(token_rows, QUERY_HEADS * HEAD_SIZE),
            "seq",
            split_axis=1,
            concat_axis=0,
            tiled=True,
        ),
        lax.all_to_all(
            key_value_reduced.reshape(token_rows, KEY_VALUE_HEADS * 2 * HEAD_SIZE),
            "seq",
            split_axis=1,
            concat_axis=0,
            tiled=True,
        ),
    )
    query_matrix = query_heads.reshape(group_rows, local_key_value, repeat_factor, HEAD_SIZE)
    keyval_group = keyval_heads.reshape(group_rows, local_key_value, 2, HEAD_SIZE)
    key_rows = keyval_group[:, :, 0]
    value_rows = keyval_group[:, :, 1]

    def scores_of(block_idx):
        row_start = block_idx * QUERY_ROWS
        query_rows = lax.dynamic_slice_in_dim(query_matrix, row_start, QUERY_ROWS, 0)
        placed_rows = lax.dynamic_slice_in_dim(placed_tokens, row_start, QUERY_ROWS, 0)
        docs_rows = lax.dynamic_slice_in_dim(documents_for_rows, row_start, QUERY_ROWS, 0)
        allowed = (docs_rows[:, None] == documents_for_rows[None, :]) & (
            placed_tokens[None, :] <= placed_rows[:, None]
        )
        raw_scores = (
            jnp.einsum("rkad,jkd->karj", query_rows, key_rows, preferred_element_type=jnp.float32)
            * factor
        )
        return (query_rows, jnp.where(allowed, raw_scores, MASKED))

    def forward_block(block_idx):
        query_rows, masked = scores_of(block_idx)
        row_top = jnp.max(masked, axis=-1, keepdims=True)
        row_total = jnp.sum(jnp.exp(masked - row_top), axis=-1, keepdims=True)
        log_total = row_top + jnp.log(row_total)
        weights_low = jnp.exp(masked - log_total).astype(jnp.bfloat16)
        block_result = jnp.einsum(
            "karj,jkd->rkad", weights_low, value_rows, preferred_element_type=jnp.float32
        )
        return (block_result.astype(jnp.bfloat16), log_total)

    head_outs, log_totals = lax.map(forward_block, jnp.arange(count_blocks))
    attended = lax.all_to_all(
        head_outs.reshape(group_rows, local_key_value * repeat_factor * HEAD_SIZE),
        "seq",
        split_axis=0,
        concat_axis=1,
        tiled=True,
    )
    middle = hidden + plain_product(attended, out_w)
    ffn_in = normed(middle, ffn_gain).astype(jnp.bfloat16)
    gate_all, up_all, down_all = (
        lax.all_gather(w_gate, "dp", axis=1, tiled=True),
        lax.all_gather(w_up, "dp", axis=1, tiled=True),
        lax.all_gather(w_down, "dp", axis=0, tiled=True),
    )
    gate_pre = plain_product(ffn_in, gate_all)
    up_pre = plain_product(ffn_in, up_all)
    activated = (jax.nn.silu(gate_pre) * up_pre).astype(jnp.bfloat16)
    ffn_result = plain_product(activated, down_all)
    block_output = (middle + ffn_result).astype(jnp.bfloat16)
    upstream = cotangent.astype(jnp.float32)
    grad_act = dot_right_t(cotangent, down_all)
    grad_down_part = dot_left_t(activated, cotangent)
    grad_gate, grad_up = gate_back(gate_pre, up_pre, grad_act)
    grad_gate_part = dot_left_t(ffn_in, grad_gate)
    grad_up_part = dot_left_t(ffn_in, grad_up)
    grad_ffn_in = dot_right_t(grad_gate, gate_all) + dot_right_t(grad_up, up_all)
    grad_gate_w, grad_up_w, grad_down = (
        lax.psum_scatter(
            grad_gate_part.astype(jnp.bfloat16), "dp", scatter_dimension=1, tiled=True
        ).astype(jnp.float32),
        lax.psum_scatter(
            grad_up_part.astype(jnp.bfloat16), "dp", scatter_dimension=1, tiled=True
        ).astype(jnp.float32),
        lax.psum_scatter(
            grad_down_part.astype(jnp.bfloat16), "dp", scatter_dimension=0, tiled=True
        ).astype(jnp.float32),
    )
    grad_middle_add, ffn_gain_terms = norm_back(middle, ffn_gain, grad_ffn_in)
    grad_ffn_gain = jnp.sum(ffn_gain_terms, axis=0)
    grad_middle = upstream + grad_middle_add
    grad_branch = grad_middle.astype(jnp.bfloat16)
    grad_out_w = dot_left_t(attended, grad_branch)
    grad_attended = dot_right_t(grad_branch, out_w).astype(jnp.bfloat16)
    grad_head_outs = lax.all_to_all(grad_attended, "seq", split_axis=1, concat_axis=0, tiled=True)
    grad_outs_all = grad_head_outs.reshape(group_rows, local_key_value, repeat_factor, HEAD_SIZE)

    def backward_block(carried, group_members):
        grad_keys, grad_values = carried
        block_idx, log_total = group_members
        query_rows, masked = scores_of(block_idx)
        weights_full = jnp.exp(masked - log_total)
        weights_low = weights_full.astype(jnp.bfloat16)
        grad_rows = lax.dynamic_slice_in_dim(grad_outs_all, block_idx * QUERY_ROWS, QUERY_ROWS, 0)
        grad_weights = jnp.einsum(
            "rkad,jkd->karj", grad_rows, value_rows, preferred_element_type=jnp.float32
        )
        row_dot = jnp.sum(weights_full * grad_weights, axis=-1, keepdims=True)
        grad_scores = (weights_full * (grad_weights - row_dot)).astype(jnp.bfloat16)
        grad_query_rows = (
            jnp.einsum("karj,jkd->rkad", grad_scores, key_rows, preferred_element_type=jnp.float32)
            * factor
        )
        grad_keys = (
            grad_keys
            + jnp.einsum(
                "karj,rkad->jkd", grad_scores, query_rows, preferred_element_type=jnp.float32
            )
            * factor
        )
        grad_values = grad_values + jnp.einsum(
            "karj,rkad->jkd", weights_low, grad_rows, preferred_element_type=jnp.float32
        )
        return ((grad_keys, grad_values), grad_query_rows.astype(jnp.bfloat16))

    zero_heads = jnp.zeros((group_rows, local_key_value, HEAD_SIZE), jnp.float32)
    (grad_keys, grad_values), grad_query_blocks = lax.scan(
        backward_block, (zero_heads, zero_heads), (jnp.arange(count_blocks), log_totals)
    )
    grad_query_heads = grad_query_blocks.reshape(
        group_rows, local_key_value * repeat_factor * HEAD_SIZE
    )
    grad_keyval_heads = (
        jnp.stack([grad_keys, grad_values], axis=2)
        .astype(jnp.bfloat16)
        .reshape(group_rows, local_key_value * 2 * HEAD_SIZE)
    )
    grad_query_tok, key_value_gradient_tokens = (
        lax.all_to_all(grad_query_heads, "seq", split_axis=0, concat_axis=1, tiled=True),
        lax.all_to_all(grad_keyval_heads, "seq", split_axis=0, concat_axis=1, tiled=True),
    )
    grad_query_rot = rotate(
        grad_query_tok.reshape(token_rows, QUERY_HEADS, HEAD_SIZE).astype(jnp.float32),
        angle_cos,
        -angle_sin,
    )
    grad_query_raw, query_gain_terms = norm_back(query_raw, query_gain, grad_query_rot)
    grad_query_gain = jnp.sum(query_gain_terms, axis=(0, 1))
    key_value_gradient_split = key_value_gradient_tokens.reshape(
        token_rows, KEY_VALUE_HEADS, 2, HEAD_SIZE
    )
    grad_key_rot = rotate(
        key_value_gradient_split[:, :, 0].astype(jnp.float32), angle_cos, -angle_sin
    )
    grad_key_raw, key_gain_terms = norm_back(key_value_unrotated[:, :, 0], key_gain, grad_key_rot)
    grad_key_gain = jnp.sum(key_gain_terms, axis=(0, 1))
    grad_query_low = grad_query_raw.astype(jnp.bfloat16).reshape(
        token_rows, QUERY_HEADS * HEAD_SIZE
    )
    grad_keyval_low = jnp.stack(
        [grad_key_raw.astype(jnp.bfloat16), key_value_gradient_split[:, :, 1]], axis=2
    ).reshape(token_rows, KEY_VALUE_HEADS * 2 * HEAD_SIZE)
    grad_normed_in = dot_right_t(grad_query_low, query_w) + dot_right_t(
        grad_keyval_low, key_value_matrix
    )
    grad_query_w = dot_left_t(normalized_input, grad_query_low)
    grad_keyval_w = dot_left_t(normalized_input, grad_keyval_low)
    grad_hidden_add, attn_gain_terms = norm_back(hidden, attn_gain, grad_normed_in)
    grad_attn_gain = jnp.sum(attn_gain_terms, axis=0)
    grad_hidden = grad_middle + grad_hidden_add
    (
        owned_attn_gain,
        owned_query_w,
        owned_keyval_w,
        owned_query_gain,
        owned_key_gain,
        owned_out_w,
        owned_ffn_gain,
    ) = (
        lax.psum_scatter(
            grad_attn_gain.astype(jnp.bfloat16), "dp", scatter_dimension=0, tiled=True
        ).astype(jnp.float32),
        lax.psum_scatter(
            grad_query_w.astype(jnp.bfloat16), "dp", scatter_dimension=0, tiled=True
        ).astype(jnp.float32),
        lax.psum_scatter(
            grad_keyval_w.astype(jnp.bfloat16), "dp", scatter_dimension=0, tiled=True
        ).astype(jnp.float32),
        lax.psum_scatter(
            grad_query_gain.astype(jnp.bfloat16), "dp", scatter_dimension=0, tiled=True
        ).astype(jnp.float32),
        lax.psum_scatter(
            grad_key_gain.astype(jnp.bfloat16), "dp", scatter_dimension=0, tiled=True
        ).astype(jnp.float32),
        lax.psum_scatter(
            grad_out_w.astype(jnp.bfloat16), "dp", scatter_dimension=0, tiled=True
        ).astype(jnp.float32),
        lax.psum_scatter(
            grad_ffn_gain.astype(jnp.bfloat16), "dp", scatter_dimension=0, tiled=True
        ).astype(jnp.float32),
    )
    (
        total_attn_gain,
        total_query_w,
        total_keyval_w,
        total_query_gain,
        total_key_gain,
        total_out_w,
        total_ffn_gain,
        total_gate_w,
        total_up_w,
        total_down_w,
    ) = lax.psum(
        (
            owned_attn_gain,
            owned_query_w,
            owned_keyval_w,
            owned_query_gain,
            owned_key_gain,
            owned_out_w,
            owned_ffn_gain,
            grad_gate_w,
            grad_up_w,
            grad_down,
        ),
        "seq",
    )
    return (
        block_output,
        grad_hidden,
        total_attn_gain,
        total_query_w,
        total_keyval_w,
        total_query_gain,
        total_key_gain,
        total_out_w,
        total_ffn_gain,
        total_gate_w,
        total_up_w,
        total_down_w,
    )


def solution(mesh):
    return jax.shard_map(
        shards,
        mesh=mesh,
        in_specs=(
            P(("dp", "seq"), None),
            P("dp"),
            P("dp", None),
            P("dp", None),
            P("dp"),
            P("dp"),
            P("dp", None),
            P("dp"),
            P(None, "dp"),
            P(None, "dp"),
            P("dp", None),
            P(("dp", "seq"), None),
            P("dp", None),
            P("dp", None),
        ),
        out_specs=(
            P(("dp", "seq"), None),
            P(("dp", "seq"), None),
            P("dp"),
            P("dp", None),
            P("dp", None),
            P("dp"),
            P("dp"),
            P("dp", None),
            P("dp"),
            P(None, "dp"),
            P(None, "dp"),
            P("dp", None),
        ),
        check_vma=False,
    )
```

profile of v0, /device:TPU:8, one launch (start us, length us, event | category | flops | bytes accessed | tf_op | source)
XLA Modules:
  0.0 1338.1 jit_solution(3187364560856251971)
XLA Ops:
  22.0 14.6 %all-reduce.8 = (bf16[64]{0:T(256)(128)(2,1)S(1)}, bf16[64]{0:T(256)(128)(2,1)S(1)}) all-reduce(bf16[64]{0:T(256)(128)(2,1)S(1)} %dynamic-update-slice, bf16[64]{0:T(256)(128)(2,1)S(1)} %dynamic-update-slice.1), channel_id=1, replica_groups=mesh['dp'=8,'seq'=4] {'dp'}, use_global_device_ids=true, to_apply=%add | all-reduce | flops 128 | bytes 512
  37.3 11.8 gather_fusion.1
  80.3 11.8 gather_fusion
  102.5 61.7 %while.28 = (s32[]{:T(128)}, bf16[4,512,2,2,64]{1,4,3,2,0:T(8,128)(2,1)}, f32[4,2,2,512,1]{3,2,1,4,0:T(2,128)}, s32[4]{0:T(128)S(1)}, s32[2048]{0:T(1024)S(1)}, ...) while((s32[]{:T(128)}, ...), condition=%wide.region_8.9_spmd.clone, body=%wide.region_5.8_spmd.clone.sunk | while | flops 1123155968 | bytes 56201496 | solution.py:189
  168.6 12.5 all-gather.1
  189.8 10.1 fusion.93
  199.9 80.6 %all-gather.17.cloned.1.call-done = bf16[1024,4608]{0,1:T(8,128)(2,1)} async-done(((bf16[1024,576]{0,1:T(8,128)(2,1)}), bf16[1024,4608]{0,1:T(8,128)(2,1)}) %all-gather.17.cloned.1.call-update) | async-done | bytes 9437200 | tf_op jit(solution)/shard_map/all_gather | solution.py:201
  280.5 10.2 fusion.94
  290.7 80.5 %all-gather.19.cloned.1.call-done = bf16[4608,1024]{1,0:T(8,128)(2,1)} async-done(((bf16[576,1024]{1,0:T(8,128)(2,1)}), bf16[4608,1024]{1,0:T(8,128)(2,1)}) %all-gather.19.cloned.1.call-update) | async-done | bytes 9437200 | tf_op jit(solution)/shard_map/all_gather | solution.py:202
  371.2 18.5 %multiply_convert_fusion = (bf16[512,4608]{1,0:T(8,128)(2,1)}, bf16[512,4608]{1,0:T(8,128)(2,1)}, bf16[512,4608]{1,0:T(8,128)(2,1)}) fusion(f32[512,4608]{1,0:T(8,128)} %fusion.93, f32[512,4608]{1,0:T(8,128)} %fusion.94, bf16[512,1024]{1,0:T(8,128)(2,1)} %param.29, bf16[4608,1024]{1,0:T(8,128)(2,1)} %all-gather.19.cloned.1.call-done), kind=kOutput, calls=%fused_computation.69 | convolution fusion | flops 4869586944 | bytes 43515904 | tf_op jit(solution)/shard_map/dot_general | solution.py:71
  389.7 9.6 fusion.95
  418.2 9.8 all-to-all-done.3
  434.4 199.1 %while.29 = (s32[]{:T(128)}, f32[2048,2,64]{0,2,1:T(8,128)}, f32[2048,2,64]{0,2,1:T(8,128)}, bf16[4,512,2,2,64]{1,4,3,2,0:T(8,128)(2,1)}, s32[4]{0:T(128)S(1)}, ...) while((s32[]{:T(128)}, f32[2048,2,64]{0,2,1:T(8,128)}, ...), condition=%wide.region_13.14_spmd.clone, body=%wide.region_11.13_spmd.clone.sunk | while | flops 2751987712 | bytes 254768080 | solution.py:265
  442.1 11.6 fusion.160
  453.6 10.9 fusion.161
  491.6 11.5 fusion.160
  503.1 10.9 fusion.161
  541.3 11.5 fusion.160
  552.8 10.9 fusion.161
  591.0 11.5 fusion.160
  602.6 10.9 fusion.161
  639.4 11.2 all-to-all-done.4
  668.3 16.0 %all_to_all.90 = bf16[4,512,256]{1,2,0:T(8,128)(2,1)S(1)} all-to-all(bf16[4,512,256]{1,2,0:T(8,128)(2,1)S(1)} %copy.108), channel_id=1, replica_groups=mesh['dp'=8,'seq'=4] {'seq'}, dimensions={0} | all-to-all | bytes 2097152 | tf_op jit(solution)/shard_map/all_to_all | solution.py:278
  691.9 10.0 convolution_convert_fusion.2
  702.0 10.2 convolution_convert_fusion.1
  713.4 10.0 convolution_convert_fusion
  725.0 9.9 add_convert_fusion
  741.4 13.4 %all-reduce.7 = (bf16[1024]{0:T(1024)(128)(2,1)S(1)}, bf16[64]{0:T(256)(128)(2,1)S(1)}, bf16[64]{0:T(256)(128)(2,1)S(1)}, bf16[1024]{0:T(1024)(128)(2,1)S(1)}) all-reduce(bf16[1024]{0:T(1024)(128)(2,1)S(1)} %get-tuple-element.224, bf16[64]{0:T(256)(128)(2,1)S(1)} %reduce_sum.160, ...), channel_id=2, replica_groups=mesh['dp'=8,'seq'=4] {'dp'}, use_global_device_ids=true, to_apply=%region_18.19.clone | all-reduce | flops 2176 | bytes 8704
  758.6 78.1 %reduce-scatter.13.cloned.1.call-done = bf16[1024,576]{0,1:T(8,128)(2,1)} async-done(((bf16[1024,4608]{0,1:T(8,128)(2,1)}), bf16[1024,576]{0,1:T(8,128)(2,1)}) %reduce-scatter.13.cloned.1.call-update) | async-done | bytes 1179664 | tf_op jit(solution)/shard_map/reduce_scatter | solution.py:217
  836.7 99.8 %reduce-scatter.15.cloned.1.call-done = bf16[1024,576]{0,1:T(8,128)(2,1)} async-done(((bf16[1024,4608]{0,1:T(8,128)(2,1)}), bf16[1024,576]{0,1:T(8,128)(2,1)}) %reduce-scatter.15.cloned.1.call-update) | async-done | bytes 1179664 | tf_op jit(solution)/shard_map/reduce_scatter | solution.py:220
  936.5 100.1 %reduce-scatter.17.cloned.1.call-done = bf16[576,1024]{1,0:T(8,128)(2,1)} async-done(((bf16[4608,1024]{1,0:T(8,128)(2,1)}), bf16[576,1024]{1,0:T(8,128)(2,1)}) %reduce-scatter.17.cloned.1.call-update) | async-done | bytes 1179664 | tf_op jit(solution)/shard_map/reduce_scatter | solution.py:223
  1036.6 294.2 %all-reduce.10 = (f32[128]{0:T(128)}, f32[128,1024]{1,0:T(8,128)}, f32[128,1024]{1,0:T(8,128)}, f32[8]{0:T(128)}, f32[8]{0:T(128)}, /*index=5*/f32[128,1024]{1,0...) all-reduce(f32[128]{0:T(128)S(1)} %dynamic-slice_convert_fusion.4, ...), channel_id=1, replica_groups=mesh['dp'=8,'seq'=4] {'seq'}, use_global_device_ids=true, to_apply=%region_19.20 | all-reduce | flops 2162960 | bytes 12978304 | tf_op jit(solution)/shard_map/psum | solution.py:351
  (448 shorter events, 301.2 us)
Async XLA Ops:
  7.2 14.3 %copy-start.56 = (bf16[8]{0:T(256)(128)(2,1)S(1)}, bf16[8]{0:T(256)(128)(2,1)}, u32[]{:S(2)}) copy-start(bf16[8]{0:T(256)(128)(2,1)} %param.22) | copy-start | bytes 52
  7.2 14.6 %copy-start.57 = (bf16[8]{0:T(256)(128)(2,1)S(1)}, bf16[8]{0:T(256)(128)(2,1)}, u32[]{:S(2)}) copy-start(bf16[8]{0:T(256)(128)(2,1)} %param.23) | copy-start | bytes 52
  7.2 29.9 %copy-start.58 = (s32[1,16]{1,0:T(1,128)S(1)}, s32[1,16]{1,0:T(1,128)}, u32[]{:S(2)}) copy-start(s32[1,16]{1,0:T(1,128)} %param.31) | copy-start | bytes 196
  7.2 43.2 %all-gather.9.cloned.1.call-start = ((), (), s32[]{:S(2)}) async-start(), calls=%async_computation.12 | async-start | bytes 2359296 | tf_op jit(solution)/shard_map/all_gather | solution.py:115
  8.0 62.5 %all-gather.11.cloned.1.call-start = ((), (), s32[]{:S(2)}) async-start(), calls=%async_computation.13 | async-start | bytes 2359296 | tf_op jit(solution)/shard_map/all_gather | solution.py:116
  8.7 172.4 %all-gather.13.cloned.1.call-start = ((), (), s32[]{:S(2)}) async-start(), calls=%async_computation.14 | async-start | bytes 2359296 | tf_op jit(solution)/shard_map/all_gather | solution.py:119
  9.5 180.3 %all-gather.15.cloned.1.call-start = ((), (), s32[]{:S(2)}) async-start(), calls=%async_computation.15 | async-start | bytes 10616832 | tf_op jit(solution)/shard_map/all_gather | solution.py:200
  10.0 270.4 %all-gather.17.cloned.1.call-start = ((), (), s32[]{:S(2)}) async-start(), calls=%async_computation.16 | async-start | bytes 10616832 | tf_op jit(solution)/shard_map/all_gather | solution.py:201
  20.3 50.2 %copy-start.40 = (f32[8,1,128]{2,1,0:T(1,128)}, f32[8,1,128]{2,1,0:T(1,128)S(1)}, u32[]{:S(2)}) copy-start(f32[8,1,128]{2,1,0:T(1,128)S(1)} %convert_element_type.218) | copy-start | bytes 12292
  36.6 20.3 %copy-start.46 = (f32[64]{0:T(128)}, f32[64]{0:T(128)S(1)}, u32[]{:S(2)}) copy-start(f32[64]{0:T(128)S(1)} %convert_element_type.174) | copy-start | bytes 772
  36.7 37.1 %copy-start.44 = (f32[64]{0:T(128)}, f32[64]{0:T(128)S(1)}, u32[]{:S(2)}) copy-start(f32[64]{0:T(128)S(1)} %convert_element_type.177) | copy-start | bytes 772
  49.5 21.0 %copy-start.42 = (f32[512]{0:T(512)}, f32[512]{0:T(512)S(1)}, u32[]{:S(2)}) copy-start(f32[512]{0:T(512)S(1)} %add_rsqrt_fusion.3) | copy-start | bytes 6148
  50.4 24.4 %copy-start.21 = (f32[512,32]{0,1:T(8,128)}, f32[512,32]{0,1:T(8,128)S(1)}, u32[]{:S(2)}) copy-start(f32[512,32]{0,1:T(8,128)S(1)} %get-tuple-element.315) | copy-start | bytes 196612
  59.4 16.7 %all-to-all-start = ((bf16[512,4,256]{0,2,1:T(8,128)(2,1)}), bf16[512,4,256]{0,2,1:T(8,128)(2,1)S(1)}, u32[]{:S(2)}, u32[]{:S(2)}) async-start(bf16[512,4,256]{0,2,1:T(8,128)(2,1)} %bitcast.11), calls=%async_computation | async-start | bytes 2097152 | tf_op jit(solution)/shard_map/all_to_all | solution.py:144
  76.1 19.6 %all-to-all-start.1 = ((bf16[512,4,256]{0,2,1:T(8,128)(2,1)}), bf16[512,4,256]{0,2,1:T(8,128)(2,1)S(1)}, u32[]{:S(2)}, u32[]{:S(2)}) async-start(bf16[512,4,256]{0,2,1:T(8,128)(2,1)} %bitcast.17), calls=%async_computation.1 | async-start | bytes 2097152 | tf_op jit(solution)/shard_map/all_to_all | solution.py:151
  79.8 291.4 %all-gather.19.cloned.1.call-start = ((), (), s32[]{:S(2)}) async-start(), calls=%async_computation.17 | async-start | bytes 10616832 | tf_op jit(solution)/shard_map/all_gather | solution.py:202
  164.2 18.7 %all-to-all-start.2 = ((bf16[4,512,256]{1,2,0:T(8,128)(2,1)}), bf16[4,512,256]{1,2,0:T(8,128)(2,1)}, u32[]{:S(2)}, u32[]{:S(2)}) async-start(bf16[4,512,256]{1,2,0:T(8,128)(2,1)} %bitcast.312), calls=%async_computation.2 | async-start | bytes 2097152 | tf_op jit(solution)/shard_map/all_to_all | solution.py:190
  409.3 18.7 %all-to-all-start.3 = ((bf16[512,4,256]{2,0,1:T(8,128)(2,1)}), bf16[512,4,256]{2,0,1:T(8,128)(2,1)}, u32[]{:S(2)}, u32[]{:S(2)}) async-start(bf16[512,4,256]{2,0,1:T(8,128)(2,1)} %bitcast.310), calls=%async_computation.3 | async-start | bytes 2097152 | tf_op jit(solution)/shard_map/all_to_all | solution.py:233
  413.6 345.0 %reduce-scatter.11.cloned.1.call-start = ((), (), s32[]{:S(2)}) async-start(), calls=%async_computation.20 | async-start | bytes 2359296 | tf_op jit(solution)/shard_map/reduce_scatter | solution.py:333
  439.4 14.2 %copy-start.1 = (f32[2,512,2,2048]{3,1,2,0:T(8,128)}, f32[2,512,2,2048]{3,1,2,0:T(8,128)S(1)}, u32[]{:S(2)}) copy-start(f32[2,512,2,2048]{3,1,2,0:T(8,128)S(1)} %fusion.159) | copy-start | bytes 50331652 | tf_op jit(solution)/shard_map/while
  464.5 14.6 %slice-start = ((s8[8388608]{0:T(1024)(128)(4,1)}), s8[4194304]{0:T(1024)(128)(4,1)S(1)}, s32[]{:S(2)}) async-start(s8[8388608]{0:T(1024)(128)(4,1)} %bitcast.295), calls=%async_computation.24 | async-start | bytes 8388608 | tf_op jit(solution)/shard_map/while
  514.0 14.8 %slice-start = ((s8[8388608]{0:T(1024)(128)(4,1)}), s8[4194304]{0:T(1024)(128)(4,1)S(1)}, s32[]{:S(2)}) async-start(s8[8388608]{0:T(1024)(128)(4,1)} %bitcast.295), calls=%async_computation.24 | async-start | bytes 8388608 | tf_op jit(solution)/shard_map/while
  563.7 14.8 %slice-start = ((s8[8388608]{0:T(1024)(128)(4,1)}), s8[4194304]{0:T(1024)(128)(4,1)S(1)}, s32[]{:S(2)}) async-start(s8[8388608]{0:T(1024)(128)(4,1)} %bitcast.295), calls=%async_computation.24 | async-start | bytes 8388608 | tf_op jit(solution)/shard_map/while
  588.4 14.2 %copy-start.1 = (f32[2,512,2,2048]{3,1,2,0:T(8,128)}, f32[2,512,2,2048]{3,1,2,0:T(8,128)S(1)}, u32[]{:S(2)}) copy-start(f32[2,512,2,2048]{3,1,2,0:T(8,128)S(1)} %fusion.159) | copy-start | bytes 50331652 | tf_op jit(solution)/shard_map/while
  613.5 14.8 %slice-start = ((s8[8388608]{0:T(1024)(128)(4,1)}), s8[4194304]{0:T(1024)(128)(4,1)S(1)}, s32[]{:S(2)}) async-start(s8[8388608]{0:T(1024)(128)(4,1)} %bitcast.295), calls=%async_computation.24 | async-start | bytes 8388608 | tf_op jit(solution)/shard_map/while
  633.5 17.1 %all-to-all-start.4 = ((bf16[4,512,256]{1,2,0:T(8,128)(2,1)}), bf16[4,512,256]{1,2,0:T(8,128)(2,1)S(1)}, u32[]{:S(2)}, u32[]{:S(2)}) async-start(bf16[4,512,256]{1,2,0:T(8,128)(2,1)} %bitcast.311), calls=%async_computation.4 | async-start | bytes 2097152 | tf_op jit(solution)/shard_map/all_to_all | solution.py:277
  637.1 121.5 %reduce-scatter.7.cloned.1.call-start = ((), (), s32[]{:S(2)}) async-start(), calls=%async_computation.18 | async-start | bytes 2359296 | tf_op jit(solution)/shard_map/reduce_scatter | solution.py:321
  665.5 93.1 %reduce-scatter.9.cloned.1.call-start = ((), (), s32[]{:S(2)}) async-start(), calls=%async_computation.19 | async-start | bytes 2359296 | tf_op jit(solution)/shard_map/reduce_scatter | solution.py:324
  690.7 146.0 %reduce-scatter.13.cloned.1.call-start = ((), (), s32[]{:S(2)}) async-start(), calls=%async_computation.21 | async-start | bytes 10616832 | tf_op jit(solution)/shard_map/reduce_scatter | solution.py:217
  702.0 234.6 %reduce-scatter.15.cloned.1.call-start = ((), (), s32[]{:S(2)}) async-start(), calls=%async_computation.22 | async-start | bytes 10616832 | tf_op jit(solution)/shard_map/reduce_scatter | solution.py:220
  712.2 324.4 %reduce-scatter.17.cloned.1.call-start = ((), (), s32[]{:S(2)}) async-start(), calls=%async_computation.23 | async-start | bytes 10616832 | tf_op jit(solution)/shard_map/reduce_scatter | solution.py:223
  738.4 16.8 %copy-start.19 = (f32[512,1024]{1,0:T(8,128)S(1)}, f32[512,1024]{1,0:T(8,128)}, u32[]{:S(2)}) copy-start(f32[512,1024]{1,0:T(8,128)} %copy-done.18) | copy-start | bytes 6291460
  (100 other events, 474.6 us)
Sparse Core Ops, SparseCore 0:
  9.7 30.5 all-gather.8
  41.9 28.5 all-gather.10
  72.1 28.5 all-gather.12
  102.2 87.5 all-gather.14
  191.3 89.1 all-gather.16
  282.0 89.1 all-gather.18
  418.3 33.8 reduce-scatter.10
  665.7 32.2 reduce-scatter.6
  700.3 34.5 reduce-scatter.8
  737.0 99.7 reduce-scatter.12
  839.0 97.4 reduce-scatter.14
  938.7 97.8 reduce-scatter.16
where the time goes:
time: 1350 us; the launch traced here: 1340 us
  waiting for transfers between devices  474 us (35%)
  blocking collectives  360 us (27%)
  matrix products  293 us (22%)
  other arithmetic  94.1 us (7%)
  local copies, waits for them, and re-layouts  73.3 us (5%)
  starting transfers between devices  20.2 us (1%)
  between operations  17.5 us (1%)
    psum x1, blocking collectives, shards(): lax.psum((owned_attn_gain, owned_query_w, owned_keyval_w, owned_query_gai...  294 us
    reduce_scatter x1, waiting for transfers between devices, shards(): lax.psum_scatter(grad_down_part.astype(jnp.bfloat16), 'dp', scatter_dimen...  100 us
    reduce_scatter x1, waiting for transfers between devices, shards(): lax.psum_scatter(grad_up_part.astype(jnp.bfloat16), 'dp', scatter_dimensi...  99.8 us
    all_gather x1, waiting for transfers between devices, shards(): lax.all_gather(w_up, 'dp', axis=1, tiled=True)  80.6 us
    all_gather x1, waiting for transfers between devices, shards(): lax.all_gather(w_down, 'dp', axis=0, tiled=True)  80.5 us
    reduce_scatter x1, waiting for transfers between devices, shards(): lax.psum_scatter(grad_gate_part.astype(jnp.bfloat16), 'dp', scatter_dimen...  78.1 us
    dot_general x4, matrix products, backward_block(): jnp.einsum('rkad,jkd->karj', grad_rows, value_rows, preferred_element_typ...  46.1 us
    convert_element_type x4, other arithmetic, backward_block(): grad_scores = (weights_full * (grad_weights - row_dot)).astype(jnp.bfloat16)  43.6 us
  transfers between devices with their start and end apart: 17, of which 10 were waited for; matrix products, arithmetic and copies ran while one was open for 31% of the time, Pallas kernels for 0%

commit v1 on v0

--- a/solution.py
+++ b/solution.py
@@ -12,6 +12,18 @@
 EPS = 1e-05
 THETA = 1000000.0
 MASKED = -1e30
+
+
+def doubled_up(array, axis, dim):
+    ways, here, lap = (lax.axis_size(axis), lax.axis_index(axis), array.shape[dim])
+    line, have = (array, 1)
+    while have < ways:
+        line = jnp.concatenate(
+            [line, lax.ppermute(line, axis, [(d, (d - have) % ways) for d in range(ways)])],
+            axis=dim,
+        )
+        have = 2 * have
+    return jnp.roll(line, here * lap, axis=dim)
 
 
 def normed(tensor, gain_vec):
@@ -199,7 +211,7 @@
     gate_all, up_all, down_all = (
         lax.all_gather(w_gate, "dp", axis=1, tiled=True),
         lax.all_gather(w_up, "dp", axis=1, tiled=True),
-        lax.all_gather(w_down, "dp", axis=0, tiled=True),
+        doubled_up(w_down, "dp", 0),
     )
     gate_pre = plain_product(ffn_in, gate_all)
     up_pre = plain_product(ffn_in, up_all)

time: 1350 us -> 1550 us (1.15)
  blocking collectives: 360 us -> 569 us
  waiting for transfers between devices: 474 us -> 398 us
  local copies, waits for them, and re-layouts: 73.3 us -> 113 us
    all_gather x1, blocking collectives: 12.5 us -> 196 us  [shards(): lax.all_gather(norm_ffn, 'dp', axis=0, tiled=True)]
    ppermute x0 -> x3, waiting for transfers between devices: none -> 98.4 us  [doubled_up(): lax.ppermute(line, axis, [(d, (d - have) % ways) for d in range(ways)])]
    all_gather x1, waiting for transfers between devices: 80.6 us -> 0.01 us  [shards(): lax.all_gather(w_up, 'dp', axis=1, tiled=True)]
    all_gather x1 -> x0, waiting for transfers between devices: 80.5 us -> none  [shards(): lax.all_gather(w_down, 'dp', axis=0, tiled=True)]
    all_gather x1, blocking collectives: 9 us -> 35.3 us  [shards(): lax.all_gather(norm_attn, 'dp', axis=0, tiled=True)]
  transfers between devices with their start and end apart: 17 -> 19, of which waited for: 10 -> 7; matrix products, arithmetic and copies ran while one was open for 31% -> 31% of each run, Pallas kernels for 0% -> 0%
where the time goes in v1:
time: 1550 us; the launch traced here: 1540 us
  blocking collectives  569 us (37%)
  waiting for transfers between devices  398 us (26%)
  matrix products  301 us (19%)
  local copies, waits for them, and re-layouts  113 us (7%)
  other arithmetic  109 us (7%)
  starting transfers between devices  24.5 us (2%)
  between operations  17.1 us (1%)
    psum x1, blocking collectives, shards(): lax.psum((owned_attn_gain, owned_query_w, owned_keyval_w, owned_query_gai...  294 us
    all_gather x1, blocking collectives, shards(): lax.all_gather(norm_ffn, 'dp', axis=0, tiled=True)  196 us
    reduce_scatter x1, waiting for transfers between devices, shards(): lax.psum_scatter(grad_down_part.astype(jnp.bfloat16), 'dp', scatter_dimen...  100 us
    reduce_scatter x1, waiting for transfers between devices, shards(): lax.psum_scatter(grad_up_part.astype(jnp.bfloat16), 'dp', scatter_dimensi...  100 us
    ppermute x3, waiting for transfers between devices, doubled_up(): lax.ppermute(line, axis, [(d, (d - have) % ways) for d in range(ways)])  98.4 us
    reduce_scatter x1, waiting for transfers between devices, shards(): lax.psum_scatter(grad_gate_part.astype(jnp.bfloat16), 'dp', scatter_dimen...  71.4 us
    dot_general x4, matrix products, backward_block(): jnp.einsum('rkad,jkd->karj', grad_rows, value_rows, preferred_element_typ...  46 us
    convert_element_type x4, other arithmetic, backward_block(): grad_scores = (weights_full * (grad_weights - row_dot)).astype(jnp.bfloat16)  43.7 us
  transfers between devices with their start and end apart: 19, of which 7 were waited for; matrix products, arithmetic and copies ran while one was open for 31% of the time, Pallas kernels for 0%

profile of v1, /device:TPU:8, one launch (start us, length us, event | category | flops | bytes accessed | tf_op | source)
XLA Modules:
  0.0 1537.7 jit_solution(15737162873994259671)
XLA Ops:
  10.6 35.3 %all-gather = bf16[8,1,128]{2,1,0:T(2,128)(2,1)S(1)} all-gather(bf16[1,1,128]{2,1,0:T(2,128)(2,1)} %bitcast.336), channel_id=1, replica_groups=mesh['dp'=8,'seq'=4] {'dp'}, dimensions={0}, use_global_device_ids=true | all-gather | bytes 2304 | tf_op jit(solution)/shard_map/all_gather | solution.py:126
  49.6 14.9 all-reduce.8
  67.4 11.8 gather_fusion.1
  79.2 20.5 %gather_fusion = s32[2048]{0:T(1024)} fusion(s32[2048]{0:T(1024)S(1)} %bitcast.305, s32[2048]{0:T(1024)S(1)} %get-tuple-element.325), kind=kCustom, calls=%fused_computation | custom fusion | bytes 24576 | tf_op jit(solution)/shard_map/gather | solution.py:75
  135.8 98.4 %collective-permute-done.1 = bf16[1152,1024]{1,0:T(8,128)(2,1)} collective-permute-done((bf16[1152,1024]{1,0:T(8,128)(2,1)}, bf16[1152,1024]{1,0:T(8,128)(2,1)}, u32[]{:S(2)}, u32[]{:S(2)}) %collective-permute-start.1) | collective-permute-done | bytes 2359328 | tf_op jit(solution)/shard_map/ppermute | solution.py:22
  247.6 69.8 %while.28 = (s32[]{:T(128)}, bf16[4,512,2,2,64]{1,4,3,2,0:T(8,128)(2,1)}, f32[4,2,2,512,1]{3,2,1,4,0:T(2,128)}, s32[4]{0:T(128)S(1)}, s32[2048]{0:T(1024)}, /*in...) while((s32[]{:T(128)}, ...), condition=%wide.region_8.9_spmd.clone, body=%wide.region_5.8_spmd.clone.sunk | while | flops 1123155968 | bytes 56202504 | solution.py:201
  321.7 195.9 %all-gather.1 = bf16[8,1,128]{2,1,0:T(2,128)(2,1)S(1)} all-gather(bf16[1,1,128]{2,1,0:T(2,128)(2,1)S(1)} %bitcast.337), channel_id=1, replica_groups=mesh['dp'=8,'seq'=4] {'dp'}, dimensions={0}, use_global_device_ids=true | all-gather | bytes 2304 | tf_op jit(solution)/shard_map/all_gather | solution.py:132
  546.2 11.4 fusion.106
  557.5 11.1 fusion.107
  568.7 17.4 %fusion.66 = (bf16[512,4608]{1,0:T(8,128)(2,1)}, bf16[512,4608]{1,0:T(8,128)(2,1)}, bf16[512,4608]{1,0:T(8,128)(2,1)}) fusion(f32[512,4608]{1,0:T(8,128)} %fusion.106, f32[512,4608]{1,0:T(8,128)} %fusion.107, bf16[512,1024]{1,0:T(8,128)(2,1)} %param.29, bf16[9216,1024]{1,0:T(8,128)(2,1)} %constant_dynamic-update-slice_fusion, s32[]{:T(128)S(6)} %select_n.60), kind=kOutput, calls=%fused_computation.75 | convolution fusion | flops 4869586944 | bytes 43515908 | tf_op jit(solution)/shard_map/dot_general | solution.py:83
  586.1 9.3 fusion.108
  613.8 9.7 all-to-all-done.3
  628.9 210.6 %while.29 = (s32[]{:T(128)}, f32[2048,2,64]{0,2,1:T(8,128)}, f32[2048,2,64]{0,2,1:T(8,128)}, bf16[4,512,2,2,64]{1,4,3,2,0:T(8,128)(2,1)}, s32[4]{0:T(128)S(1)}, ...) while((s32[]{:T(128)}, f32[2048,2,64]{0,2,1:T(8,128)}, ...), condition=%wide.region_13.14_spmd.clone, body=%wide.region_11.13_spmd.clone.sunk | while | flops 2751987712 | bytes 288191712 | solution.py:277
  638.3 11.5 fusion.171
  649.8 10.9 fusion.172
  690.3 11.5 fusion.171
  701.9 10.9 fusion.172
  743.0 11.5 fusion.171
  754.5 10.9 fusion.172
  795.7 11.5 fusion.171
  807.2 10.9 fusion.172
  843.4 16.6 %all_to_all.90 = bf16[4,512,256]{1,2,0:T(8,128)(2,1)S(1)} all-to-all(bf16[4,512,256]{1,2,0:T(8,128)(2,1)S(1)} %copy.114), channel_id=1, replica_groups=mesh['dp'=8,'seq'=4] {'seq'}, dimensions={0} | all-to-all | bytes 2097152 | tf_op jit(solution)/shard_map/all_to_all | solution.py:290
  871.7 10.0 all-to-all-done.4
  899.2 10.0 convolution_convert_fusion.2
  909.2 10.3 convolution_convert_fusion.1
  920.7 10.0 convolution_convert_fusion
  932.3 9.9 add_convert_fusion
  948.8 12.5 all-reduce.7
  965.1 71.4 %reduce-scatter.13.cloned.1.call-done = bf16[1024,576]{0,1:T(8,128)(2,1)} async-done(((bf16[1024,4608]{0,1:T(8,128)(2,1)}), bf16[1024,576]{0,1:T(8,128)(2,1)}) %reduce-scatter.13.cloned.1.call-update) | async-done | bytes 1179664 | tf_op jit(solution)/shard_map/reduce_scatter | solution.py:229
  1036.5 100.0 %reduce-scatter.15.cloned.1.call-done = bf16[1024,576]{0,1:T(8,128)(2,1)} async-done(((bf16[1024,4608]{0,1:T(8,128)(2,1)}), bf16[1024,576]{0,1:T(8,128)(2,1)}) %reduce-scatter.15.cloned.1.call-update) | async-done | bytes 1179664 | tf_op jit(solution)/shard_map/reduce_scatter | solution.py:232
  1136.5 100.2 %reduce-scatter.17.cloned.1.call-done = bf16[576,1024]{1,0:T(8,128)(2,1)} async-done(((bf16[4608,1024]{1,0:T(8,128)(2,1)}), bf16[576,1024]{1,0:T(8,128)(2,1)}) %reduce-scatter.17.cloned.1.call-update) | async-done | bytes 1179664 | tf_op jit(solution)/shard_map/reduce_scatter | solution.py:235
  1236.7 294.2 %all-reduce.10 = (f32[128]{0:T(128)}, f32[128,1024]{1,0:T(8,128)}, f32[128,1024]{1,0:T(8,128)}, f32[8]{0:T(128)}, f32[8]{0:T(128)}, /*index=5*/f32[128,1024]{1,0...) all-reduce(f32[128]{0:T(128)S(1)} %dynamic-slice_convert_fusion.4, ...), channel_id=1, replica_groups=mesh['dp'=8,'seq'=4] {'seq'}, use_global_device_ids=true, to_apply=%region_19.20 | all-reduce | flops 2162960 | bytes 12978304 | tf_op jit(solution)/shard_map/psum | solution.py:363
  (399 shorter events, 343.8 us)
Async XLA Ops:
  7.2 100.7 %all-gather.10.cloned.1.call-start = ((), (), s32[]{:S(2)}) async-start(), calls=%async_computation.13 | async-start | bytes 2359296 | tf_op jit(solution)/shard_map/all_gather | solution.py:128
  7.9 110.5 %all-gather.8.cloned.1.call-start = ((), (), s32[]{:S(2)}) async-start(), calls=%async_computation.12 | async-start | bytes 2359296 | tf_op jit(solution)/shard_map/all_gather | solution.py:127
  8.7 515.8 %all-gather.12.cloned.1.call-start = ((), (), s32[]{:S(2)}) async-start(), calls=%async_computation.14 | async-start | bytes 2359296 | tf_op jit(solution)/shard_map/all_gather | solution.py:131
  9.4 536.8 %all-gather.14.cloned.1.call-start = ((), (), s32[]{:S(2)}) async-start(), calls=%async_computation.15 | async-start | bytes 10616832 | tf_op jit(solution)/shard_map/all_gather | solution.py:212
  10.0 547.6 %all-gather.16.cloned.1.call-start = ((), (), s32[]{:S(2)}) async-start(), calls=%async_computation.16 | async-start | bytes 10616832 | tf_op jit(solution)/shard_map/all_gather | solution.py:213
  10.0 92.3 %collective-permute-start = (bf16[576,1024]{1,0:T(8,128)(2,1)}, bf16[576,1024]{1,0:T(8,128)(2,1)S(1)}, u32[]{:S(2)}, u32[]{:S(2)}) collective-permute-start(bf16[576,1024]{1,0:T(8,128)(2,1)} %param.28), channel_id=1, source_target_pairs={{0,28},{4,0},{8,4},{12,8},{16,12},{20,16},{24,20},{28,24},{1,29},{... | collective-permute-start | bytes 3538952 | tf_op jit(solution)/shard_map/ppermute | solution.py:22
  45.8 72.6 %copy-start.39 = (f32[8,1,128]{2,1,0:T(1,128)}, f32[8,1,128]{2,1,0:T(1,128)S(1)}, u32[]{:S(2)}) copy-start(f32[8,1,128]{2,1,0:T(1,128)S(1)} %convert_element_type.218) | copy-start | bytes 12292
  64.5 46.9 %copy-start.43 = (f32[64]{0:T(128)}, f32[64]{0:T(128)S(1)}, u32[]{:S(2)}) copy-start(f32[64]{0:T(128)S(1)} %convert_element_type.177) | copy-start | bytes 772
  67.2 57.9 %copy-start.45 = (f32[64]{0:T(128)}, f32[64]{0:T(128)S(1)}, u32[]{:S(2)}) copy-start(f32[64]{0:T(128)S(1)} %convert_element_type.174) | copy-start | bytes 772
  79.2 23.1 %copy-start.9 = (bf16[576,1024]{1,0:T(8,128)(2,1)S(1)}, bf16[576,1024]{1,0:T(8,128)(2,1)}, u32[]{:S(2)}) copy-start(bf16[576,1024]{1,0:T(8,128)(2,1)} %param.28) | copy-start | bytes 3538948
  101.4 17.1 %copy-start.41 = (f32[512]{0:T(512)}, f32[512]{0:T(512)S(1)}, u32[]{:S(2)}) copy-start(f32[512]{0:T(512)S(1)} %add_rsqrt_fusion.3) | copy-start | bytes 6148
  102.3 23.3 %copy-start.25 = (f32[512,32]{0,1:T(8,128)}, f32[512,32]{0,1:T(8,128)S(1)}, u32[]{:S(2)}) copy-start(f32[512,32]{0,1:T(8,128)S(1)} %get-tuple-element.315) | copy-start | bytes 196612
  104.1 130.1 %collective-permute-start.1 = (bf16[1152,1024]{1,0:T(8,128)(2,1)}, bf16[1152,1024]{1,0:T(8,128)(2,1)}, u32[]{:S(2)}, u32[]{:S(2)}) collective-permute-start(bf16[1152,1024]{1,0:T(8,128)(2,1)} %pad_maximum_fusion.1), channel_id=1, source_target_pairs={{0,24},{4,28},{8,0},{12,4},{16,8},{20,12},{24,16},{28,20},{1,25},{... | collective-permute-start | bytes 7077896 | tf_op jit(solution)/shard_map/ppermute | solution.py:22
  114.2 17.7 %all-to-all-start.1 = ((bf16[512,4,256]{0,2,1:T(8,128)(2,1)}), bf16[512,4,256]{0,2,1:T(8,128)(2,1)}, u32[]{:S(2)}, u32[]{:S(2)}) async-start(bf16[512,4,256]{0,2,1:T(8,128)(2,1)} %bitcast.17), calls=%async_computation.1 | async-start | bytes 2097152 | tf_op jit(solution)/shard_map/all_to_all | solution.py:163
  131.8 111.1 %all-to-all-start = ((bf16[512,4,256]{0,2,1:T(8,128)(2,1)}), bf16[512,4,256]{0,2,1:T(8,128)(2,1)S(1)}, u32[]{:S(2)}, u32[]{:S(2)}) async-start(bf16[512,4,256]{0,2,1:T(8,128)(2,1)} %bitcast.11), calls=%async_computation | async-start | bytes 2097152 | tf_op jit(solution)/shard_map/all_to_all | solution.py:156
  238.0 292.5 %collective-permute-start.2 = (bf16[2304,1024]{1,0:T(8,128)(2,1)}, bf16[2304,1024]{1,0:T(8,128)(2,1)}, u32[]{:S(2)}, u32[]{:S(2)}) collective-permute-start(bf16[2304,1024]{1,0:T(8,128)(2,1)} %pad_maximum_fusion), channel_id=1, source_target_pairs={{0,16},{4,20},{8,24},{12,28},{16,0},{20,4},{24,8},{28,12},{1,17},{... | collective-permute-start | bytes 14155784 | tf_op jit(solution)/shard_map/ppermute | solution.py:22
  247.6 74.1 %copy-start.48 = (bf16[128]{0:T(256)(128)(2,1)S(1)}, bf16[128]{0:T(256)(128)(2,1)}, u32[]{:S(2)}) copy-start(bf16[128]{0:T(256)(128)(2,1)} %param.25) | copy-start | bytes 772
  317.5 207.0 %all-to-all-start.2 = ((bf16[4,512,256]{1,2,0:T(8,128)(2,1)}), bf16[4,512,256]{1,2,0:T(8,128)(2,1)}, u32[]{:S(2)}, u32[]{:S(2)}) async-start(bf16[4,512,256]{1,2,0:T(8,128)(2,1)} %bitcast.320), calls=%async_computation.2 | async-start | bytes 2097152 | tf_op jit(solution)/shard_map/all_to_all | solution.py:202
  605.7 17.8 %all-to-all-start.3 = ((bf16[512,4,256]{2,0,1:T(8,128)(2,1)}), bf16[512,4,256]{2,0,1:T(8,128)(2,1)S(1)}, u32[]{:S(2)}, u32[]{:S(2)}) async-start(bf16[512,4,256]{2,0,1:T(8,128)(2,1)} %bitcast.319), calls=%async_computation.3 | async-start | bytes 2097152 | tf_op jit(solution)/shard_map/all_to_all | solution.py:245
  609.2 355.9 %reduce-scatter.11.cloned.1.call-start = ((), (), s32[]{:S(2)}) async-start(), calls=%async_computation.19 | async-start | bytes 2359296 | tf_op jit(solution)/shard_map/reduce_scatter | solution.py:345
  613.8 351.3 %reduce-scatter.9.cloned.1.call-start = ((), (), s32[]{:S(2)}) async-start(), calls=%async_computation.18 | async-start | bytes 2359296 | tf_op jit(solution)/shard_map/reduce_scatter | solution.py:336
  842.3 17.9 %copy-start.26 = (f32[512,32]{0,1:T(8,128)S(1)}, f32[512,32]{0,1:T(8,128)}, u32[]{:S(2)}) copy-start(f32[512,32]{0,1:T(8,128)} %copy-done.25) | copy-start | bytes 196612
  842.3 17.9 %copy-start.34 = (f32[512,32]{0,1:T(8,128)S(1)}, f32[512,32]{0,1:T(8,128)}, u32[]{:S(2)}) copy-start(f32[512,32]{0,1:T(8,128)} %get-tuple-element.313) | copy-start | bytes 196612
  843.1 17.2 %copy-start.18 = (f32[512,1024]{0,1:T(8,128)S(1)}, f32[512,1024]{0,1:T(8,128)}, u32[]{:S(2)}) copy-start(f32[512,1024]{0,1:T(8,128)} %copy-done.17) | copy-start | bytes 6291460
  843.1 17.2 %copy-start.38 = (f32[512,8]{0,1:T(8,128)S(1)}, f32[512,8]{0,1:T(8,128)}, u32[]{:S(2)}) copy-start(f32[512,8]{0,1:T(8,128)} %copy-done.37) | copy-start | bytes 49156
  843.2 17.2 %copy-start.44 = (f32[64]{0:T(128)S(1)}, f32[64]{0:T(128)}, u32[]{:S(2)}) copy-start(f32[64]{0:T(128)} %copy-done.43) | copy-start | bytes 772
  865.2 16.5 %all-to-all-start.4 = ((bf16[4,512,256]{1,2,0:T(8,128)(2,1)}), bf16[4,512,256]{1,2,0:T(8,128)(2,1)}, u32[]{:S(2)}, u32[]{:S(2)}) async-start(bf16[4,512,256]{1,2,0:T(8,128)(2,1)} %bitcast.29), calls=%async_computation.4 | async-start | bytes 2097152 | tf_op jit(solution)/shard_map/all_to_all | solution.py:289
  869.4 95.6 %reduce-scatter.7.cloned.1.call-start = ((), (), s32[]{:S(2)}) async-start(), calls=%async_computation.17 | async-start | bytes 2359296 | tf_op jit(solution)/shard_map/reduce_scatter | solution.py:333
  899.1 137.4 %reduce-scatter.13.cloned.1.call-start = ((), (), s32[]{:S(2)}) async-start(), calls=%async_computation.20 | async-start | bytes 10616832 | tf_op jit(solution)/shard_map/reduce_scatter | solution.py:229
  909.2 227.4 %reduce-scatter.15.cloned.1.call-start = ((), (), s32[]{:S(2)}) async-start(), calls=%async_computation.21 | async-start | bytes 10616832 | tf_op jit(solution)/shard_map/reduce_scatter | solution.py:232
  919.5 317.2 %reduce-scatter.17.cloned.1.call-start = ((), (), s32[]{:S(2)}) async-start(), calls=%async_computation.22 | async-start | bytes 10616832 | tf_op jit(solution)/shard_map/reduce_scatter | solution.py:235
  945.7 15.9 %copy-start.23 = (f32[512,1024]{1,0:T(8,128)S(1)}, f32[512,1024]{1,0:T(8,128)}, u32[]{:S(2)}) copy-start(f32[512,1024]{1,0:T(8,128)} %copy-done.22) | copy-start | bytes 6291460
  (73 other events, 440.2 us)
Sparse Core Ops, SparseCore 0:
  9.6 36.7 all-gather.9
  48.0 30.1 all-gather.7
  79.8 28.6 all-gather.11
  109.9 126.8 all-gather.13
  238.3 215.4 all-gather.15
  613.9 33.6 reduce-scatter.10
  865.3 31.5 reduce-scatter.8
  899.7 34.7 reduce-scatter.6
  936.8 99.5 reduce-scatter.12
  1038.6 97.8 reduce-scatter.14
  1138.8 97.8 reduce-scatter.16
